TPU v7x, 32 devices: a whole 2x2x4 slice. The times are simulated.
32 devices in a mesh: node: 8 (over z, x), mp: 4 (over y, core).
Axes of the slice: x: 2, y: 2, z: 4, core: 2. Of those that a mesh axis runs over, the one named last changes fastest.
Arguments:
- queries: bfloat16 [32, 64, 128], P('node', 'mp'), may hold values from -8 to 8
- root_keys: bfloat16 [16384, 8, 128], P('node', 'mp'), may hold values from -6 to 6
- root_values: bfloat16 [16384, 8, 128], P('node', 'mp'), may hold values from -6 to 6
- mid_keys: bfloat16 [8, 1024, 8, 128], P('node', None, 'mp'), may hold values from -6 to 6
- mid_values: bfloat16 [8, 1024, 8, 128], P('node', None, 'mp'), may hold values from -6 to 6
- leaf_keys: bfloat16 [32, 256, 8, 128], P('node', None, 'mp'), may hold values from -6 to 6
- leaf_values: bfloat16 [32, 256, 8, 128], P('node', None, 'mp'), may hold values from -6 to 6
- mid_length: int32 [8], replicated, may hold values from 1 to 1024
- leaf_length: int32 [32], P('node'), may hold values from 1 to 256
- branch_mid: int32 [32, 1], replicated, may hold values from 0 to 7; in each aligned block of 32 rows (0 to 31, 32 to 63, ...) at most 8 rows name the same one
- residual: bfloat16 [32, 8192], P(None, 'node'), may hold values from -6 to 6
- norm_gain: float32 [8192], P('node'), may hold values from 0.5 to 1.5
- out_weight: bfloat16 [8192, 8192], P('mp', 'node'), may hold values from -0.0625 to 0.0625
- gate_weight: bfloat16 [8192, 28672], P('node', 'mp'), may hold values from -0.0625 to 0.0625
- up_weight: bfloat16 [8192, 28672], P('node', 'mp'), may hold values from -0.0625 to 0.0625
- down_weight: bfloat16 [28672, 8192], P('mp', 'node'), may hold values from -0.03125 to 0.03125
Outputs:
- layer_out: bfloat16 [32, 8192], P('mp', 'node')
Inputs may be any that keep to these rules, and one draw needn't show every extreme that they name: `branch_mid`: every inner tree node lies on the path of 1 to 8 branches, and some node on exactly 8.
All inputs are finite; a program needn't handle non-finite values.
Results may differ from a plain program's by a relative error of at most 0.015.
Values may be sent and summed in bfloat16 or wider, within the bound.
A program may use at most 128 MiB of HBM per device.

v0:
```python
import jax
import jax.numpy as jnp
from jax import lax
from jax.sharding import PartitionSpec as P

D = 8192
CAP = 8


masked_score = -1e30
norm_eps = 1e-05


def partial_scores(grouped, key_block, value_block, usable, scaling):
    scores = (
        jnp.einsum("bkgd,lkd->bkgl", grouped, key_block, preferred_element_type=jnp.float32)
        * scaling
    )
    masking = usable[:, None, None, :]
    scores = jnp.where(masking, scores, masked_score)
    highest = jnp.max(scores, axis=-1)
    weights = jnp.where(masking, jnp.exp(scores - highest[..., None]), 0.0)
    weighted = jnp.einsum(
        "bkgl,lkd->bkgd",
        weights.astype(jnp.bfloat16),
        value_block,
        preferred_element_type=jnp.float32,
    )
    return (highest, jnp.sum(weights, axis=-1), weighted)


def combine_parts(earlier, later):
    highest = jnp.maximum(earlier[0], later[0])
    first_factor = jnp.exp(earlier[0] - highest)
    second_factor = jnp.exp(later[0] - highest)
    totals = earlier[1] * first_factor + later[1] * second_factor
    weighted = earlier[2] * first_factor[..., None] + later[2] * second_factor[..., None]
    return (highest, totals, weighted)


def on_device(
    queries,
    root_keys,
    root_values,
    mid_keys,
    mid_values,
    leaf_keys,
    leaf_values,
    mid_length,
    leaf_length,
    branch_mid,
    residual,
    norm_gain,
    out_weight,
    gate_weight,
    up_weight,
    down_weight,
):
    owned = queries.shape[0]
    local_heads = queries.shape[1]
    head_size = queries.shape[2]
    local_groups = root_keys.shape[1]
    group_size = local_heads // local_groups
    scaling = head_size ** (-0.5)
    node_count = lax.axis_size("node")
    gathered = lax.all_gather(queries, "node", axis=0, tiled=True)
    every_branch = gathered.shape[0]
    grouped = gathered.reshape(every_branch, local_groups, group_size, head_size)
    root_usable = jnp.ones((every_branch, root_keys.shape[0]), dtype=bool)
    root_part = partial_scores(grouped, root_keys, root_values, root_usable, scaling)
    local_mids = mid_keys.shape[0]
    node_ids = lax.axis_index("node") * local_mids + jnp.arange(local_mids, dtype=jnp.int32)
    routing = branch_mid[:, 0]
    matching = routing[None, :] == node_ids[:, None]
    ranking = jnp.cumsum(matching.astype(jnp.int32), axis=1) - 1
    selected = matching[:, None, :] & (
        ranking[:, None, :] == jnp.arange(CAP, dtype=jnp.int32)[None, :, None]
    )
    picked = jnp.einsum(
        "ncb,bkgd->nckgd",
        selected.astype(jnp.bfloat16),
        grouped,
        preferred_element_type=jnp.float32,
    ).astype(jnp.bfloat16)
    slot_index = jnp.arange(mid_keys.shape[1])

    def node_partial(inputs):
        node_queries, node_keys, node_values, node_id = inputs
        usable = jnp.broadcast_to(
            slot_index[None, :] < mid_length[node_id], (CAP, slot_index.shape[0])
        )
        return partial_scores(node_queries, node_keys, node_values, usable, scaling)

    node_high, node_totals, node_weighted = lax.map(
        node_partial, (picked, mid_keys, mid_values, node_ids)
    )
    chosen = selected.astype(jnp.float32)
    covered = jnp.sum(chosen, axis=(0, 1))
    back_high = (
        jnp.einsum("ncb,nckg->bkg", chosen, node_high, precision=lax.Precision.HIGHEST)
        + ((1.0 - covered) * masked_score)[:, None, None]
    )
    back_totals = jnp.einsum("ncb,nckg->bkg", chosen, node_totals, precision=lax.Precision.HIGHEST)
    back_weighted = jnp.einsum(
        "ncb,nckgd->bkgd", chosen, node_weighted, precision=lax.Precision.HIGHEST
    )
    shared_part = combine_parts(root_part, (back_high, back_totals, back_weighted))
    peaks, totals, weighted = (
        lax.all_to_all(shared_part[0], "node", split_axis=0, concat_axis=0, tiled=True),
        lax.all_to_all(shared_part[1], "node", split_axis=0, concat_axis=0, tiled=True),
        lax.all_to_all(shared_part[2], "node", split_axis=0, concat_axis=0, tiled=True),
    )
    peaks = peaks.reshape(node_count, owned, local_groups, group_size)
    totals = totals.reshape(node_count, owned, local_groups, group_size)
    weighted = weighted.reshape(node_count, owned, local_groups, group_size, head_size)
    highest = jnp.max(peaks, axis=0)
    factor = jnp.exp(peaks - highest[None])
    merged = (
        highest,
        jnp.sum(totals * factor, axis=0),
        jnp.sum(weighted * factor[..., None], axis=0),
    )
    own_grouped = queries.reshape(owned, local_groups, group_size, head_size)
    leaf_scores = (
        jnp.einsum("bkgd,blkd->bkgl", own_grouped, leaf_keys, preferred_element_type=jnp.float32)
        * scaling
    )
    leaf_usable = (jnp.arange(leaf_keys.shape[1])[None, :] < leaf_length[:, None])[:, None, None, :]
    leaf_scores = jnp.where(leaf_usable, leaf_scores, masked_score)
    leaf_peak = jnp.max(leaf_scores, axis=-1)
    leaf_weights = jnp.where(leaf_usable, jnp.exp(leaf_scores - leaf_peak[..., None]), 0.0)
    leaf_weighted = jnp.einsum(
        "bkgl,blkd->bkgd",
        leaf_weights.astype(jnp.bfloat16),
        leaf_values,
        preferred_element_type=jnp.float32,
    )
    final_part = combine_parts(merged, (leaf_peak, jnp.sum(leaf_weights, axis=-1), leaf_weighted))
    attended = (
        (final_part[2] / final_part[1][..., None])
        .reshape(owned, local_heads * head_size)
        .astype(jnp.bfloat16)
    )
    projected = jnp.dot(
        lax.all_gather(attended, "node", axis=0, tiled=True),
        out_weight,
        preferred_element_type=jnp.float32,
    )
    projected = lax.psum(projected.astype(jnp.bfloat16), "mp").astype(jnp.float32)
    stream = residual.astype(jnp.float32) + projected
    squares = lax.psum(jnp.sum(stream * stream, axis=1), "node")
    normed = (stream * lax.rsqrt(squares[:, None] / D + norm_eps) * norm_gain[None, :]).astype(
        jnp.bfloat16
    )
    out_rows = every_branch // lax.axis_size("mp")
    gate, upward = (
        lax.psum(
            jnp.dot(normed, gate_weight, preferred_element_type=jnp.float32).astype(jnp.bfloat16),
            "node",
        ).astype(jnp.float32),
        lax.psum(
            jnp.dot(normed, up_weight, preferred_element_type=jnp.float32).astype(jnp.bfloat16),
            "node",
        ).astype(jnp.float32),
    )
    act = (jax.nn.silu(gate) * upward).astype(jnp.bfloat16)
    mlp_rows = lax.psum_scatter(
        jnp.dot(act, down_weight, preferred_element_type=jnp.float32).astype(jnp.bfloat16),
        "mp",
        scatter_dimension=0,
        tiled=True,
    ).astype(jnp.float32)
    stream_rows = lax.dynamic_slice_in_dim(stream, lax.axis_index("mp") * out_rows, out_rows, 0)
    return (stream_rows + mlp_rows).astype(jnp.bfloat16)


def solution(mesh):
    in_specs = (
        P("node", "mp", None),
        P("node", "mp", None),
        P("node", "mp", None),
        P("node", None, "mp", None),
        P("node", None, "mp", None),
        P("node", None, "mp", None),
        P("node", None, "mp", None),
        P(),
        P("node"),
        P(),
        P(None, "node"),
        P("node"),
        P("mp", "node"),
        P("node", "mp"),
        P("node", "mp"),
        P("mp", "node"),
    )
    out_specs = P("mp", "node")
    return jax.shard_map(
        on_device, mesh=mesh, in_specs=in_specs, out_specs=out_specs, check_vma=False
    )
```

profile of v0, /device:TPU:19, one launch (start us, length us, event | category | flops | bytes accessed | tf_op | source)
XLA Modules:
  0.0 295.0 jit_solution(1106771095615868161)
XLA Ops:
  6.5 1.3 dynamic_slice.18
  7.9 0.6 iota_compare_fusion.2
  8.5 0.7 compare_bitcast_fusion
  9.5 22.8 %all_gather.6 = bf16[32,16,128]{2,1,0:T(8,128)(2,1)S(1)} all-gather(bf16[4,16,128]{2,1,0:T(8,128)(2,1)} %param.16), channel_id=1, replica_groups=mesh['node'=8,'mp'=4] {'node'}, dimensions={0}, use_global_device_ids=true | all-gather | bytes 147456 | tf_op jit(solution)/shard_map/all_gather | solution.py:66
  32.4 1.4 fusion.79
  34.2 2.1 bitcast_reduce_fusion
  36.5 1.8 copy-done.1
  38.3 0.8 fusion.1
  39.2 0.7 copy.115
  39.9 7.2 %all-to-all-start.2 = ((f32[32,2,8]{2,1,0:T(2,128)}), f32[32,2,8]{2,1,0:T(2,128)S(1)}, u32[]{:S(2)}, u32[]{:S(2)}) async-start(f32[32,2,8]{2,1,0:T(2,128)} %copy.115), calls=%async_computation.2 | async-start | bytes 65536 | tf_op jit(solution)/shard_map/all_to_all | solution.py:110
  47.2 0.3 convolution_bitcast_fusion
  47.5 3.3 %fusion.13 = f32[32,2,8,128]{3,0,2,1:T(8,128)S(1)} fusion(f32[2,2048,32,8]{1,2,3,0:T(8,128)} %copy-done.1, f32[32,2,8]{0,2,1:T(8,128)S(1)} %get-tuple-element.48, bf16[2048,2,128,1]{2,1,0,3:T(2,128)(2,1)S(1)} %bitcast.75, f32[32,2,8]{0,2,1:T(8,128)S(1)} %subtract_exponential_fusion.2), kind=kOutput, calls=%fused_computation.16 | convolution fusion | flops 271646720 | bytes 5509120 | tf_op jit(solution)/shard_map/bkgl,lkd->bkgd/dot_general | solution.py:23
  50.8 0.3 fusion.80
  51.2 0.7 copy.104
  51.9 5.6 %all-to-all-start.1 = ((f32[32,2,8]{2,1,0:T(2,128)}), f32[32,2,8]{2,1,0:T(2,128)S(1)}, u32[]{:S(2)}, u32[]{:S(2)}) async-start(f32[32,2,8]{2,1,0:T(2,128)} %copy.104), calls=%async_computation.1 | async-start | bytes 65536 | tf_op jit(solution)/shard_map/all_to_all | solution.py:109
  57.4 0.3 fusion.12
  57.8 0.8 copy.103
  58.6 1.2 all-to-all-done.1
  59.9 6.5 %all-to-all-start = ((f32[32,2,8,128]{3,2,1,0:T(8,128)}), f32[32,2,8,128]{3,2,1,0:T(8,128)S(1)}, u32[]{:S(2)}, u32[]{:S(2)}) async-start(f32[32,2,8,128]{3,2,1,0:T(8,128)} %copy.103), calls=%async_computation | async-start | bytes 524288 | tf_op jit(solution)/shard_map/all_to_all | solution.py:111
  66.6 3.2 %all-to-all-done = f32[32,2,8,128]{3,2,1,0:T(8,128)S(1)} async-done(((f32[32,2,8,128]{3,2,1,0:T(8,128)}), f32[32,2,8,128]{3,2,1,0:T(8,128)S(1)}, u32[]{:S(2)}, u32[]{:S(2)}) %all-to-all-start) | async-done | bytes 262176 | tf_op jit(solution)/shard_map/all_to_all | solution.py:111
  70.0 0.2 fusion.19
  70.2 23.6 %all-gather = bf16[8,4,2048]{2,1,0:T(4,128)(2,1)S(1)} all-gather(bf16[1,4,2048]{2,1,0:T(4,128)(2,1)S(1)} %reshape.273), channel_id=1, replica_groups=mesh['node'=8,'mp'=4] {'node'}, dimensions={0}, use_global_device_ids=true | all-gather | bytes 147456 | tf_op jit(solution)/shard_map/all_gather | solution.py:145
  93.9 3.6 %convolution_convert_fusion.3 = bf16[32,1024]{1,0:T(8,128)(2,1)} fusion(bf16[32,2048]{1,0:T(8,128)(2,1)S(1)} %reshape.274, bf16[2048,1024]{1,0:T(8,128)(2,1)} %param.28), kind=kOutput, calls=%fused_computation.20 | convolution fusion | flops 134250496 | bytes 4390912 | tf_op jit(solution)/shard_map/dot_general | solution.py:144
  97.6 48.7 %all-reduce.4.cloned.1.call-done = bf16[32,1024]{1,0:T(8,128)(2,1)} async-done(((bf16[32,1024]{1,0:T(8,128)(2,1)}), bf16[32,1024]{1,0:T(8,128)(2,1)}) %all-reduce.4.cloned.1.call-update) | async-done | bytes 65552 | tf_op jit(solution)/shard_map/psum | solution.py:149
  146.3 1.0 convert_add_fusion
  147.3 11.6 %psum.29 = f32[32]{0:T(128)S(1)} all-reduce(f32[32]{0:T(128)S(1)} %get-tuple-element.45), channel_id=1, replica_groups=mesh['node'=8,'mp'=4] {'node'}, use_global_device_ids=true, to_apply=%region_13.14 | all-reduce | flops 32 | bytes 256 | tf_op jit(solution)/shard_map/psum | solution.py:151
  158.9 8.7 %convolution_convert_fusion = bf16[32,7168]{1,0:T(8,128)(2,1)} fusion(bf16[1024,7168]{1,0:T(8,128)(2,1)} %param.30, f32[1024]{0:T(1024)S(1)} %copy-done.5, f32[32]{0:T(128)S(1)} %add_rsqrt_fusion, bf16[32,1024]{1,0:T(8,128)(2,1)} %all-reduce.4.cloned.1.call-done, bf16[32,1024]{1,0:T(8,128)(2,1)S(1)} %copy-done.2), kind=kOutput, calls=%fused_computation | convolution fusion | flops 470188032 | bytes 15274112 | tf_op jit(solution)/shard_map/dot_general | solution.py:162
  167.6 8.6 %convolution_convert_fusion.1 = bf16[32,7168]{1,0:T(8,128)(2,1)} fusion(bf16[1024,7168]{1,0:T(8,128)(2,1)} %param.29, f32[1024]{0:T(1024)S(1)} %copy-done.5, f32[32]{0:T(128)S(1)} %add_rsqrt_fusion, bf16[32,1024]{1,0:T(8,128)(2,1)S(1)} %copy-done.3, bf16[32,1024]{1,0:T(8,128)(2,1)S(1)} %copy-done.2), kind=kOutput, calls=%fused_computation.1 | convolution fusion | flops 470188032 | bytes 15274112 | tf_op jit(solution)/shard_map/dot_general | solution.py:158
  176.3 81.4 %all-reduce.6.cloned.1.call-done = (bf16[32,7168]{1,0:T(8,128)(2,1)}, bf16[32,7168]{1,0:T(8,128)(2,1)}) async-done(((bf16[32,7168]{1,0:T(8,128)(2,1)}, bf16[32,7168]{1,0:T(8,128)(2,1)}), (bf16[32,7168]{1,0:T(8,128)(2,1)}, bf16[32,7168]{1,0:T(8,128)(2,1)})) %all-reduce.6.cloned.1.call-update) | async-done | bytes 917520 | tf_op jit(solution)/shard_map/psum | solution.py:161
  257.7 8.7 %convolution_convert_fusion.2 = bf16[32,1024]{1,0:T(8,128)(2,1)} fusion(bf16[7168,1024]{1,0:T(8,128)(2,1)} %param.31, bf16[32,7168]{1,0:T(8,128)(2,1)} %get-tuple-element.23, bf16[32,7168]{1,0:T(8,128)(2,1)} %get-tuple-element.24), kind=kOutput, calls=%fused_computation.19 | convolution fusion | flops 471629824 | bytes 15663104 | tf_op jit(solution)/shard_map/dot_general | solution.py:168
  266.5 20.7 %reduce-scatter.2.cloned.1.call-done = bf16[8,1024]{1,0:T(8,128)(2,1)} async-done(((bf16[32,1024]{1,0:T(8,128)(2,1)}), bf16[8,1024]{1,0:T(8,128)(2,1)}) %reduce-scatter.2.cloned.1.call-update) | async-done | bytes 16400 | tf_op jit(solution)/shard_map/reduce_scatter | solution.py:167
  287.2 1.3 add_convert_fusion
  (53 shorter events, 1.8 us)
Async XLA Ops:
  6.5 41.0 %copy-start = (bf16[2048,2,128]{2,1,0:T(2,128)(2,1)S(1)}, bf16[2048,2,128]{2,1,0:T(2,128)(2,1)}, u32[]{:S(2)}) copy-start(bf16[2048,2,128]{2,1,0:T(2,128)(2,1)} %param.18) | copy-start | bytes 3145732
  34.2 12.9 %copy-start.9 = (s32[4]{0:T(128)S(1)}, s32[4]{0:T(128)}, u32[]{:S(2)}) copy-start(s32[4]{0:T(128)} %param.24) | copy-start | bytes 52
  34.2 13.0 %copy-start.7 = (bf16[1,1024,2,128]{3,2,1,0:T(2,128)(2,1)S(1)}, bf16[1,1024,2,128]{3,2,1,0:T(2,128)(2,1)}, u32[]{:S(2)}) copy-start(bf16[1,1024,2,128]{3,2,1,0:T(2,128)(2,1)} %param.20) | copy-start | bytes 1572868
  36.3 1.9 copy-start.1
  39.1 11.7 %copy-start.4 = (bf16[4,256,2,128]{3,2,1,0:T(2,128)(2,1)S(1)}, bf16[4,256,2,128]{3,2,1,0:T(2,128)(2,1)}, u32[]{:S(2)}) copy-start(bf16[4,256,2,128]{3,2,1,0:T(2,128)(2,1)} %param.21) | copy-start | bytes 1572868
  39.1 11.7 %copy-start.6 = (bf16[4,16,128]{2,1,0:T(8,128)(2,1)S(1)}, bf16[4,16,128]{2,1,0:T(8,128)(2,1)}, u32[]{:S(2)}) copy-start(bf16[4,16,128]{2,1,0:T(8,128)(2,1)} %param.16) | copy-start | bytes 49156
  39.9 11.9 %all-to-all-start.2 = ((f32[32,2,8]{2,1,0:T(2,128)}), f32[32,2,8]{2,1,0:T(2,128)S(1)}, u32[]{:S(2)}, u32[]{:S(2)}) async-start(f32[32,2,8]{2,1,0:T(2,128)} %copy.115), calls=%async_computation.2 | async-start | bytes 65536 | tf_op jit(solution)/shard_map/all_to_all | solution.py:110
  47.5 22.4 %copy-start.8 = (bf16[4,256,2,128]{3,2,1,0:T(2,128)(2,1)S(1)}, bf16[4,256,2,128]{3,2,1,0:T(2,128)(2,1)}, u32[]{:S(2)}) copy-start(bf16[4,256,2,128]{3,2,1,0:T(2,128)(2,1)} %param.22) | copy-start | bytes 1572868
  51.9 94.5 %copy-start.2 = (bf16[32,1024]{1,0:T(8,128)(2,1)S(1)}, bf16[32,1024]{1,0:T(8,128)(2,1)}, u32[]{:S(2)}) copy-start(bf16[32,1024]{1,0:T(8,128)(2,1)} %param.26) | copy-start | bytes 196612
  51.9 8.0 %all-to-all-start.1 = ((f32[32,2,8]{2,1,0:T(2,128)}), f32[32,2,8]{2,1,0:T(2,128)S(1)}, u32[]{:S(2)}, u32[]{:S(2)}) async-start(f32[32,2,8]{2,1,0:T(2,128)} %copy.104), calls=%async_computation.1 | async-start | bytes 65536 | tf_op jit(solution)/shard_map/all_to_all | solution.py:109
  57.4 101.5 %copy-start.5 = (f32[1024]{0:T(1024)S(1)}, f32[1024]{0:T(1024)}, u32[]{:S(2)}) copy-start(f32[1024]{0:T(1024)} %param.27) | copy-start | bytes 12292
  59.9 10.0 %all-to-all-start = ((f32[32,2,8,128]{3,2,1,0:T(8,128)}), f32[32,2,8,128]{3,2,1,0:T(8,128)S(1)}, u32[]{:S(2)}, u32[]{:S(2)}) async-start(f32[32,2,8,128]{3,2,1,0:T(8,128)} %copy.103), calls=%async_computation | async-start | bytes 524288 | tf_op jit(solution)/shard_map/all_to_all | solution.py:111
  66.3 80.0 %all-reduce.4.cloned.1.call-start = ((), (), s32[]{:S(2)}) async-start(), calls=%async_computation.4 | async-start | bytes 131072 | tf_op jit(solution)/shard_map/psum | solution.py:149
  97.6 160.2 %all-reduce.6.cloned.1.call-start = ((), (), s32[]{:S(2)}) async-start(), calls=%async_computation.6 | async-start | bytes 1835008 | tf_op jit(solution)/shard_map/psum | solution.py:161
  158.9 8.7 %copy-start.3 = (bf16[32,1024]{1,0:T(8,128)(2,1)S(1)}, bf16[32,1024]{1,0:T(8,128)(2,1)}, u32[]{:S(2)}) copy-start(bf16[32,1024]{1,0:T(8,128)(2,1)} %all-reduce.4.cloned.1.call-done) | copy-start | bytes 196612
  176.2 110.9 %reduce-scatter.2.cloned.1.call-start = ((), (), s32[]{:S(2)}) async-start(), calls=%async_computation.5 | async-start | bytes 81920 | tf_op jit(solution)/shard_map/reduce_scatter | solution.py:167
Sparse Core Ops, SparseCore 0:
  97.7 48.5 all-reduce.3
  176.4 81.3 all-reduce.5
  266.6 20.5 reduce-scatter.1
where the time goes:
time: 298 us; the launch traced here: 295 us
  waiting for transfers between devices  155 us (52%)
  blocking collectives  58.1 us (19%)
  matrix products  38 us (13%)
  starting transfers between devices  19.3 us (6%)
  between operations  13.3 us (4%)
  local copies, waits for them, and re-layouts  5.71 us (2%)
  other arithmetic  5.33 us (2%)
    psum x1, waiting for transfers between devices, on_device(): lax.psum(jnp.dot(normed, up_weight, preferred_element_type=jnp.float32).a...  81.4 us
    psum x1, waiting for transfers between devices, on_device(): lax.psum(projected.astype(jnp.bfloat16), 'mp').astype(jnp.float32)  48.7 us
    all_gather x1, blocking collectives, on_device(): lax.all_gather(attended, 'node', axis=0, tiled=True)  23.6 us
    all_gather x1, blocking collectives, on_device(): gathered = lax.all_gather(queries, 'node', axis=0, tiled=True)  22.8 us
    reduce_scatter x1, waiting for transfers between devices, on_device(): lax.psum_scatter(jnp.dot(act, down_weight, preferred_element_type=jnp.flo...  20.7 us
    psum x1, blocking collectives, on_device(): squares = lax.psum(jnp.sum(stream * stream, axis=1), 'node')  11.6 us
    dot_general x1, matrix products, on_device(): jnp.dot(act, down_weight, preferred_element_type=jnp.float32)  8.71 us
    dot_general x1, matrix products, on_device(): jnp.dot(normed, up_weight, preferred_element_type=jnp.float32)  8.67 us
  transfers between devices with their start and end apart: 6, of which 5 were waited for; matrix products, arithmetic and copies ran while one was open for 2% of the time, Pallas kernels for 0%

commit v1 on v0

v1 whole, which is shorter than its diff:
```python
import functools
import math

import jax
import jax.numpy as jnp
import numpy as np
from jax import lax
from jax.experimental import pallas as pl
from jax.experimental.pallas import tpu as pltpu
from jax.sharding import PartitionSpec as P

norm_eps = 1e-05
masked_score = -1e30
MESH = pl.DeviceIdType.MESH
ROWS = 128


def nt_dot(a, b):
    return lax.dot_general(a, b, (((1,), (1,)), ((), ())), preferred_element_type=jnp.float32)


def nn_dot(a, b):
    return jnp.dot(a, b, preferred_element_type=jnp.float32)


def layer_kernel(
    n, mp, owners, scale2,
    q_ref, mid_lo, mid_hi, leaf_lo, leaf_hi, spread_ref, order_ref, res_ref, gain_ref,
    rk_hbm, rv_hbm, mk_hbm, mv_hbm, lk_hbm, lv_hbm, ow_hbm, gw_hbm, uw_hbm, dw_hbm,
    out_ref,
    raw, keys, values, ow, gw, uw, dw,
    qall, part_send, part_recv, leaf_part, att_own, att_all, lhs, pr_own, pr_all, stream,
    sq_own, sq_all, xg, gu_send, gu_recv, act_all, acc, dn_send, dn_recv,
    kv_sem, w_sem, q_s, q_r, p_s, p_r, a_s, a_r, s_s, s_r, g_s, g_r, c_s, c_r, o_s, o_r, d_s, d_r,
):
    me = lax.axis_index("node")
    mpi = lax.axis_index("mp")
    heads, own_rows, hd = q_ref.shape
    chunk = act_all.shape[2]
    width = stream.shape[1]
    root = rk_hbm.shape[0] // heads
    mids = mk_hbm.shape[0] // heads
    leaves = lk_hbm.shape[0] // heads
    shared = root + mids

    kv_copies = []
    for side, (a, b, c) in enumerate(((rk_hbm, mk_hbm, lk_hbm), (rv_hbm, mv_hbm, lv_hbm))):
        start = 0
        for k, src in enumerate((a, b, c)):
            size = src.shape[0]
            copy = pltpu.make_async_copy(
                src, raw.at[side, pl.ds(start, size)], kv_sem.at[side * 3 + k]
            )
            copy.start()
            kv_copies.append(copy)
            start += size
    w_copies = []
    for k, (src, dst) in enumerate(((ow_hbm, ow), (gw_hbm, gw), (uw_hbm, uw), (dw_hbm, dw))):
        copy = pltpu.make_async_copy(src, dst, w_sem.at[k])
        copy.start()
        w_copies.append(copy)

    barrier = pltpu.get_barrier_semaphore()

    def greet(axis, here, count):
        def body(i, carry):
            pl.semaphore_signal(
                barrier, inc=1, device_id={axis: lax.rem(here + i, count)}, device_id_type=MESH
            )
            return carry

        lax.fori_loop(1, count, body, 0)

    greet("node", me, n)
    greet("mp", mpi, mp)
    pl.semaphore_wait(barrier, n - 1 + mp - 1)

    def remote(src, dst, send, recv, axis, peer):
        return pltpu.make_async_remote_copy(
            src_ref=src, dst_ref=dst, send_sem=send, recv_sem=recv,
            device_id={axis: peer}, device_id_type=MESH,
        )

    def peers(axis, fn):
        here, count = (me, n) if axis == "node" else (mpi, mp)

        def body(i, carry):
            fn(lax.rem(here + i, count))
            return carry

        lax.fori_loop(1, count, body, 0)

    def send_all(axis, src, dst, send, recv):
        here = me if axis == "node" else mpi
        peers(
            axis,
            lambda j: remote(src(j), dst.at[here], send.at[j], recv.at[here], axis, j).start(),
        )

    def wait_all(axis, src, dst, send, recv):
        peers(axis, lambda j: remote(src(j), dst.at[j], send.at[j], recv.at[j], axis, j).wait())

    send_all("node", lambda j: q_ref, qall, q_s, q_r)
    qall[me] = q_ref[...]

    for copy in kv_copies:
        copy.wait()
    block = spread_ref.shape[0]
    per = block // heads

    def split(i, carry):
        at = pl.ds(pl.multiple_of(i * block, block), block)
        to = pl.ds(pl.multiple_of(i * per, per), per)
        for side, dst in enumerate((keys, values)):
            rows = nn_dot(spread_ref[...], raw[side, at, :]).astype(jnp.bfloat16)
            for h in range(heads):
                dst[h, to, :] = rows[h * per:(h + 1) * per]
        return carry

    lax.fori_loop(0, raw.shape[1] // block, split, 0)

    def leaf_attend(h):
        scores = nt_dot(q_ref[h], keys[h, shared:, :])
        slot = lax.broadcasted_iota(jnp.int32, scores.shape, 1)
        seen = (slot >= leaf_lo[...]) & (slot < leaf_hi[...])
        scores = jnp.where(seen, scores, masked_score)
        peak = jnp.max(scores, axis=1, keepdims=True)
        weights = jnp.where(seen, jnp.exp2((scores - peak) * scale2), 0.0)
        total = jnp.sum(weights, axis=1, keepdims=True)
        weighted = nn_dot(weights.astype(jnp.bfloat16), values[h, shared:, :])
        lane = lax.broadcasted_iota(jnp.int32, (own_rows, hd), 1)
        leaf_part[h, :, 0:hd] = weighted
        leaf_part[h, :, hd:] = jnp.where(lane == 0, peak, total)

    for h in range(heads):
        leaf_attend(h)

    wait_all("node", lambda j: q_ref, qall, q_s, q_r)

    group = max(1, min(n, ROWS // own_rows))
    rows = group * own_rows

    def attend(i, carry):
        picks = pl.ds(i * group, group)
        at = pl.ds(pl.multiple_of(i * rows, rows), rows)
        low, high = mid_lo[at, :], mid_hi[at, :]
        for h in range(heads):
            query = qall[picks, h].reshape(rows, hd)
            root_scores = nt_dot(query, keys[h, 0:root, :])
            mid_scores = nt_dot(query, keys[h, root:shared, :])
            slot = lax.broadcasted_iota(jnp.int32, mid_scores.shape, 1)
            seen = (slot >= low) & (slot < high)
            mid_scores = jnp.where(seen, mid_scores, masked_score)
            peak = jnp.maximum(
                jnp.max(root_scores, axis=1, keepdims=True),
                jnp.max(mid_scores, axis=1, keepdims=True),
            )
            root_weights = jnp.exp2((root_scores - peak) * scale2)
            mid_weights = jnp.where(seen, jnp.exp2((mid_scores - peak) * scale2), 0.0)
            total = jnp.sum(root_weights, axis=1, keepdims=True) + jnp.sum(
                mid_weights, axis=1, keepdims=True
            )
            weighted = nn_dot(root_weights.astype(jnp.bfloat16), values[h, 0:root, :]) + nn_dot(
                mid_weights.astype(jnp.bfloat16), values[h, root:shared, :]
            )
            lane = lax.broadcasted_iota(jnp.int32, (rows, hd), 1)
            side = jnp.where(lane == 0, peak, total)
            part_send[picks, h, :, 0:hd] = weighted.reshape(group, own_rows, hd)
            part_send[picks, h, :, hd:] = side.reshape(group, own_rows, hd)
        return carry

    lax.fori_loop(0, n // group, attend, 0)
    send_all("node", lambda j: part_send.at[j], part_recv, p_s, p_r)
    part_recv[me] = part_send[me]
    wait_all("node", lambda j: part_send.at[j], part_recv, p_s, p_r)

    for h in range(heads):
        def merge(i, carry):
            peak, total, weighted = carry
            peak_i = part_recv[i, h, :, hd:hd + 1]
            total_i = part_recv[i, h, :, hd + 1:hd + 2]
            top = jnp.maximum(peak, peak_i)
            one, two = jnp.exp2((peak - top) * scale2), jnp.exp2((peak_i - top) * scale2)
            return (
                top,
                total * one + total_i * two,
                weighted * one + part_recv[i, h, :, 0:hd] * two,
            )

        first = (
            leaf_part[h, :, hd:hd + 1],
            leaf_part[h, :, hd + 1:hd + 2],
            leaf_part[h, :, 0:hd],
        )
        _, total, weighted = lax.fori_loop(0, n, merge, first)
        att_own[h] = (weighted / total).astype(jnp.bfloat16)

    send_all("node", lambda j: att_own, att_all, a_s, a_r)
    att_all[me] = att_own[...]
    wait_all("node", lambda j: att_own, att_all, a_s, a_r)

    branches = lhs.shape[0]
    size = n * own_rows // branches
    for h in range(heads):
        mixed = att_all[:, h].reshape(n * own_rows, hd)
        mixed = nn_dot(order_ref[...], mixed).astype(jnp.bfloat16)
        for g in range(size):
            first = (h * size + g) * hd
            lhs[:, first:first + hd] = mixed[g * branches:(g + 1) * branches]

    w_copies[0].wait()
    tile = math.gcd(width, 256)

    def project(i, carry):
        at = pl.ds(pl.multiple_of(i * tile, tile), tile)
        pr_own[:, at] = nn_dot(lhs[...], ow[:, at]).astype(jnp.bfloat16)
        return carry

    lax.fori_loop(0, width // tile, project, 0)
    send_all("mp", lambda j: pr_own, pr_all, o_s, o_r)
    pr_all[mpi] = pr_own[...]
    wait_all("mp", lambda j: pr_own, pr_all, o_s, o_r)
    total = pr_all[0].astype(jnp.float32)
    for k in range(1, mp):
        total = total + pr_all[k].astype(jnp.float32)
    total = res_ref[...].astype(jnp.float32) + total
    stream[...] = total
    squares = jnp.sum(total * total, axis=1, keepdims=True)
    sq_own[...] = jnp.broadcast_to(squares, sq_own.shape)
    send_all("node", lambda j: sq_own, sq_all, s_s, s_r)
    sq_all[me] = sq_own[...]
    xg[...] = (total * gain_ref[...]).astype(jnp.bfloat16)

    w_copies[1].wait()
    w_copies[2].wait()

    def gate_up(i, carry):
        j = lax.rem(me + 1 + i, owners)
        at = pl.ds(pl.multiple_of(j * chunk, 128), chunk)
        gate = nn_dot(xg[...], gw[:, at]).astype(jnp.bfloat16)
        upward = nn_dot(xg[...], uw[:, at]).astype(jnp.bfloat16)
        gu_send[j, 0] = gate
        gu_send[j, 1] = upward

        @pl.when(j != me)
        def _():
            remote(gu_send.at[j], gu_recv.at[me], g_s.at[j], g_r.at[me], "node", j).start()

        return carry

    lax.fori_loop(0, owners, gate_up, 0)
    wait_all("node", lambda j: sq_own, sq_all, s_s, s_r)

    def owner_work():
        gu_recv[me] = gu_send[me]
        peers(
            "node",
            lambda j: remote(gu_send.at[0], gu_recv.at[j], g_s.at[0], g_r.at[j], "node", j).wait_recv(),
        )
        squares = sq_all[0][:, 0:1]
        for k in range(1, n):
            squares = squares + sq_all[k][:, 0:1]
        root_mean = lax.rsqrt(squares / (width * n) + norm_eps)

        def add(i, carry):
            return (
                carry[0] + gu_recv[i, 0].astype(jnp.float32),
                carry[1] + gu_recv[i, 1].astype(jnp.float32),
            )

        zero = jnp.zeros((branches, chunk), jnp.float32)
        gate, upward = lax.fori_loop(0, n, add, (zero, zero))
        gate, upward = gate * root_mean, upward * root_mean
        act_all[me] = (gate / (1.0 + jnp.exp(-gate)) * upward).astype(jnp.bfloat16)
        send_all("node", lambda j: act_all.at[me], act_all, c_s, c_r)

    if owners == n:
        owner_work()
    else:
        pl.when(me < owners)(owner_work)

    w_copies[3].wait()
    acc[...] = jnp.zeros(acc.shape, jnp.float32)

    def down(i, carry):
        j = lax.rem(me + i, n)

        def step():
            @pl.when(j != me)
            def _():
                remote(act_all.at[j], act_all.at[j], c_s.at[j], c_r.at[j], "node", j).wait_recv()

            at = pl.ds(pl.multiple_of(j * chunk, 128), chunk)
            acc[...] += nn_dot(act_all[j], dw[at, :])

        if owners == n:
            step()
        else:
            pl.when(j < owners)(step)
        return carry

    lax.fori_loop(0, n, down, 0)

    rows_out = out_ref.shape[0]
    for k in range(mp):
        dn_send[k] = acc[k * rows_out:(k + 1) * rows_out, :].astype(jnp.bfloat16)
    send_all("mp", lambda j: dn_send.at[j], dn_recv, d_s, d_r)
    dn_recv[mpi] = dn_send[mpi]
    wait_all("mp", lambda j: dn_send.at[j], dn_recv, d_s, d_r)
    total = dn_recv[0].astype(jnp.float32)
    for k in range(1, mp):
        total = total + dn_recv[k].astype(jnp.float32)
    own = stream[pl.ds(pl.multiple_of(mpi * rows_out, rows_out), rows_out), :]
    out_ref[...] = (own + total).astype(jnp.bfloat16)

    def sent(i, carry):
        j = lax.rem(me + 1 + i, owners)

        @pl.when(j != me)
        def _():
            remote(gu_send.at[j], gu_recv.at[me], g_s.at[j], g_r.at[me], "node", j).wait_send()

        return carry

    lax.fori_loop(0, owners, sent, 0)

    def acts_sent():
        peers(
            "node",
            lambda j: remote(act_all.at[me], act_all.at[me], c_s.at[j], c_r.at[j], "node", j).wait_send(),
        )

    if owners == n:
        acts_sent()
    else:
        pl.when(me < owners)(acts_sent)


def on_device(
    n, mp,
    queries, root_keys, root_values, mid_keys, mid_values, leaf_keys, leaf_values,
    mid_length, leaf_length, branch_mid, residual, norm_gain,
    out_weight, gate_weight, up_weight, down_weight,
):
    owned, local_heads, hd = queries.shape
    heads = root_keys.shape[1]
    size = local_heads // heads
    own_rows = owned * size
    branches = owned * n
    width = residual.shape[1]
    hidden = gate_weight.shape[1]
    lane_tiles = hidden // 128
    owners = max(k for k in range(1, n + 1) if lane_tiles % k == 0)
    chunk = hidden // owners
    mid_slots = mid_keys.shape[1]
    leaf_slots = leaf_keys.shape[1]
    local_mids = mid_keys.shape[0]

    q = queries.reshape(owned, heads, size, hd).transpose(1, 0, 2, 3).reshape(heads, own_rows, hd)
    local = branch_mid[:, 0] - lax.axis_index("node") * local_mids
    here = (local >= 0) & (local < local_mids)
    mid_lo = jnp.where(here, local * mid_slots, 0)
    mid_hi = jnp.where(here, mid_lo + mid_length[branch_mid[:, 0]], 0)
    mid_lo = jnp.repeat(mid_lo, size)[:, None]
    mid_hi = jnp.repeat(mid_hi, size)[:, None]
    leaf_lo = jnp.arange(owned, dtype=jnp.int32) * leaf_slots
    leaf_hi = jnp.repeat(leaf_lo + leaf_length, size)[:, None]
    leaf_lo = jnp.repeat(leaf_lo, size)[:, None]

    block = 128 * heads
    spread = np.zeros((block, block), np.float32)
    at = np.arange(block)
    spread[(at % heads) * 128 + at // heads, at] = 1.0
    order = np.zeros((branches * size, branches * size), np.float32)
    at = np.arange(branches * size)
    order[(at % size) * branches + at // size, at] = 1.0

    flat = [
        a.reshape(-1, hd)
        for a in (root_keys, root_values, mid_keys, mid_values, leaf_keys, leaf_values)
    ]
    raw_rows = flat[0].shape[0] + flat[2].shape[0] + flat[4].shape[0]
    bf, f32 = jnp.bfloat16, jnp.float32
    dma = pltpu.SemaphoreType.DMA
    vmem = pl.BlockSpec(memory_space=pltpu.VMEM)
    hbm = pl.BlockSpec(memory_space=pl.ANY)
    rows_out = branches // mp
    scratch = [
        pltpu.VMEM((2, raw_rows, hd), bf),
        pltpu.VMEM((heads, raw_rows // heads, hd), bf),
        pltpu.VMEM((heads, raw_rows // heads, hd), bf),
        pltpu.VMEM(out_weight.shape, bf),
        pltpu.VMEM(gate_weight.shape, bf),
        pltpu.VMEM(up_weight.shape, bf),
        pltpu.VMEM(down_weight.shape, bf),
        pltpu.VMEM((n, heads, own_rows, hd), bf),
        pltpu.VMEM((n, heads, own_rows, 2 * hd), f32),
        pltpu.VMEM((n, heads, own_rows, 2 * hd), f32),
        pltpu.VMEM((heads, own_rows, 2 * hd), f32),
        pltpu.VMEM((heads, own_rows, hd), bf),
        pltpu.VMEM((n, heads, own_rows, hd), bf),
        pltpu.VMEM((branches, local_heads * hd), bf),
        pltpu.VMEM((branches, width), bf),
        pltpu.VMEM((mp, branches, width), bf),
        pltpu.VMEM((branches, width), f32),
        pltpu.VMEM((branches, 128), f32),
        pltpu.VMEM((n, branches, 128), f32),
        pltpu.VMEM((branches, width), bf),
        pltpu.VMEM((owners, 2, branches, chunk), bf),
        pltpu.VMEM((n, 2, branches, chunk), bf),
        pltpu.VMEM((owners, branches, chunk), bf),
        pltpu.VMEM((branches, width), f32),
        pltpu.VMEM((mp, rows_out, width), bf),
        pltpu.VMEM((mp, rows_out, width), bf),
        dma((6,)),
        dma((4,)),
    ] + [dma((n,))] * 12 + [dma((mp,))] * 4
    scale2 = hd ** -0.5 * math.log2(math.e)
    return pl.pallas_call(
        functools.partial(layer_kernel, n, mp, owners, scale2),
        out_shape=jax.ShapeDtypeStruct((rows_out, width), bf),
        in_specs=[vmem] * 9 + [hbm] * 10,
        out_specs=vmem,
        scratch_shapes=scratch,
        compiler_params=pltpu.CompilerParams(
            collective_id=0, has_side_effects=True, vmem_limit_bytes=67043328
        ),
    )(
        q, mid_lo, mid_hi, leaf_lo, leaf_hi,
        jnp.asarray(spread, bf), jnp.asarray(order, bf), residual, norm_gain[None, :],
        *flat, out_weight, gate_weight, up_weight, down_weight,
    )


def solution(mesh):
    in_specs = (
        P("node", "mp", None),
        P("node", "mp", None),
        P("node", "mp", None),
        P("node", None, "mp", None),
        P("node", None, "mp", None),
        P("node", None, "mp", None),
        P("node", None, "mp", None),
        P(),
        P("node"),
        P(),
        P(None, "node"),
        P("node"),
        P("mp", "node"),
        P("node", "mp"),
        P("node", "mp"),
        P("mp", "node"),
    )
    body = functools.partial(on_device, mesh.shape["node"], mesh.shape["mp"])
    return jax.shard_map(
        body, mesh=mesh, in_specs=in_specs, out_specs=P("mp", "node"), check_vma=False
    )
```

time: 298 us -> 105 us (0.35); the launches traced: 295 us -> 105 us
  waiting for transfers between devices: 155 us -> 0 us
  Pallas kernels: 0 us -> 95.9 us
  blocking collectives: 58.1 us -> 0 us
  matrix products: 38 us -> 0 us
  starting transfers between devices: 19.3 us -> 0 us
  between operations: 13.3 us -> 0.02 us
  other arithmetic: 5.33 us -> 1.99 us
    psum x2 -> x0, waiting for transfers between devices: 130 us -> none  [the longest x1 81.4 us: on_device(): lax.psum(jnp.dot(normed, up_weight, preferred_element_type=jnp.float32).a...]
    pallas_call x0 -> x1, Pallas kernels: none -> 95.9 us  [on_device(): pl.pallas_call(functools.partial(layer_kernel, n, mp, owners, scale2), ou...]
    all_gather x2 -> x0, blocking collectives: 46.4 us -> none  [the longest x1 23.6 us: on_device(): lax.all_gather(attended, 'node', axis=0, tiled=True)]
    dot_general x12 -> x0, matrix products: 37.7 us -> none  [the longest x1 8.71 us: on_device(): jnp.dot(act, down_weight, preferred_element_type=jnp.float32)]
    reduce_scatter x1 -> x0, waiting for transfers between devices: 20.7 us -> none  [on_device(): lax.psum_scatter(jnp.dot(act, down_weight, preferred_element_type=jnp.flo...]
    all_to_all x3 -> x0, starting transfers between devices: 19.2 us -> none  [the longest x1 7.23 us: on_device(): lax.all_to_all(shared_part[1], 'node', split_axis=0, concat_axis=0, tiled...]
    psum x1 -> x0, blocking collectives: 11.6 us -> none  [on_device(): squares = lax.psum(jnp.sum(stream * stream, axis=1), 'node')]
    all_to_all x3 -> x0, waiting for transfers between devices: 4.46 us -> none  [the longest x1 3.21 us: on_device(): lax.all_to_all(shared_part[2], 'node', split_axis=0, concat_axis=0, tiled...]
  transfers between devices with their start and end apart: 6 -> 0, of which waited for: 5 -> 0; matrix products, arithmetic and copies ran while one was open for 2% -> 0% of each run, Pallas kernels for 0% -> 0%
where the time goes in v1:
time: 105 us
  Pallas kernels  95.9 us (91%)
  local copies, waits for them, and re-layouts  7.13 us (7%)
  other arithmetic  1.99 us (2%)
    pallas_call x1, Pallas kernels, on_device(): pl.pallas_call(functools.partial(layer_kernel, n, mp, owners, scale2), ou...  95.9 us

profile of v1, /device:TPU:19, one launch (start us, length us, event | category | flops | bytes accessed | tf_op | source)
XLA Modules:
  0.0 105.1 jit_solution(5305765897236295571)
XLA Ops:
  0.0 0.7 fusion.1
  0.7 0.7 fusion
  1.3 0.1 broadcast_in_dim.21
  1.4 0.1 broadcast_in_dim.22
  1.5 1.4 %gather_fusion = s32[32]{0:T(128)S(1)} fusion(s32[8]{0:T(128)} %param.25, s32[1024]{0:T(1024)S(1)} %pad_clamp_fusion), kind=kCustom, calls=%fused_computation | custom fusion | bytes 384 | tf_op jit(solution)/shard_map/gather | solution.py:363
  2.8 0.7 bitcast_select_fusion
  3.5 0.7 broadcast_in_dim_reshape.19.leaf_hi
  4.2 0.7 broadcast_in_dim_reshape.18.leaf_lo
  4.8 0.1 broadcast_in_dim.20
  4.9 0.1 broadcast_in_dim.19
  5.0 1.3 %copy_bitcast_fusion.q_ref = bf16[2,32,128]{2,1,0:T(8,128)(2,1)} fusion(bf16[4,16,128]{2,1,0:T(8,128)(2,1)} %param.18), kind=kLoop, calls=%fused_computation.1 | loop fusion | bytes 32768 | tf_op jit(solution)/shard_map/reshape | solution.py:359
  6.3 0.7 broadcast_in_dim_reshape.16.mid_lo
  7.1 0.7 broadcast_in_dim_reshape.17.mid_hi
  7.8 95.9 %shard_map.172 = bf16[8,1024]{1,0:T(8,128)(2,1)} custom-call(bf16[2,32,128]{2,1,0:T(8,128)(2,1)} %copy_bitcast_fusion.q_ref, s32[256,1]{1,0:T(8,128)} %broadcast_in_dim_reshape.16.mid_lo, s32[256,1]{1,0:T(8,128)} %broadcast_in_dim_reshape.17.mid_hi, s32[32,1]{1,0:T(8,128)} %broadcast_in_dim_reshape.18.leaf_lo, s32[32,1]{1,0:T(8,128)} %broadcast_in_dim_reshape.19.leaf_hi, ...), custom_call_target="tpu_custom_call" | custom-call | tf_op jit(solution)/shard_map/pallas_call | solution.py:419
  103.7 1.3 %copy.29 = bf16[8,1024]{1,0:T(8,128)(2,1)} copy(bf16[8,1024]{1,0:T(8,128)(2,1)} %shard_map.172) | data formatting | bytes 32768
  (2 shorter events, 0.0 us)
